TPU v7x, 256 devices: a whole 4x4x8 slice. The times are simulated.
256 devices in a mesh: pb: 32 (over x, y, z_lo), row: 8 (over z_hi, core).
Axes of the slice: x: 4, y: 4, z: 8 (z_hi: 4, z_lo: 2; z = z_hi * 2 + z_lo), core: 2. Of those that a mesh axis runs over, the one named last changes fastest.
Arguments:
- query_desc: bfloat16 [16384, 512], P(('pb', 'row')), may hold values from -6 to 6
- ref_desc: bfloat16 [12288, 512], P(('row', 'pb')), may hold values from -6 to 6
- taps: float32 [2, 8], replicated, may hold values from -1.3 to 1.3
Outputs:
- aligned: float32 [16384, 12288], P('pb', 'row')
All inputs are finite; a program needn't handle non-finite values.
Results may differ from a plain program's by a relative error of at most 0.0003.
Values may be sent and summed in bfloat16 or wider, within the bound.
No kernel may reach another device: no remote copies, remote signals or barrier semaphores. Data moves between devices by JAX's collectives and lax.ppermute only.
A program may use at most 64 MiB of HBM per device.

v0:
```python
import jax
import jax.numpy as jnp
from jax import lax
from jax.sharding import PartitionSpec as P

DESC = 512
DILATION_STEP = 32
TAP_COUNT = 8


def padded(value, sides, width):
    for axis, dim in sides:
        count, length = (lax.axis_size(axis), value.shape[dim])
        up = [(i, (i + 1) % count) for i in range(count - 1)]
        down = [(j, i) for i, j in up]
        last = lax.slice_in_dim(value, length - width, length, axis=dim)
        leading = lax.slice_in_dim(value, 0, width, axis=dim)
        before = lax.ppermute(last, axis, up)
        after = lax.ppermute(leading, axis, down)
        value = jnp.concatenate([before, value, after], axis=dim)
    return value


def diagonal_pass(padded_matrix, tap_weights, output_rows, output_columns):
    total_reach = jnp.zeros((output_rows, output_columns), jnp.float32)
    for tap_index in range(TAP_COUNT):
        total_reach = (
            total_reach
            + tap_weights[tap_index]
            * padded_matrix[
                tap_index * DILATION_STEP : tap_index * DILATION_STEP + output_rows,
                tap_index * DILATION_STEP : tap_index * DILATION_STEP + output_columns,
            ]
        )
    return jnp.tanh(total_reach)


def inner_scores(left, right):
    return lax.dot_general(
        left, right, (((1,), (1,)), ((), ())), preferred_element_type=jnp.float32
    )


def pass_rims(receptive_field):
    return padded(receptive_field, (("pb", 0), ("row", 1)), TAP_COUNT * DILATION_STEP // 2)


def local(query_desc, ref_desc, taps):
    scale = DESC ** (-0.5)
    queries = lax.all_gather(query_desc, "row", axis=0, tiled=True)
    rows = queries.shape[0]
    cols = ref_desc.shape[0] * lax.axis_size("pb")
    sim = inner_scores(queries, lax.all_gather(ref_desc, "pb", axis=0, tiled=True))
    base = jnp.tanh(sim * scale)
    first = diagonal_pass(pass_rims(base), taps[0], rows, cols)
    return diagonal_pass(pass_rims(first), taps[1], rows, cols)


def solution(mesh):
    in_specs = (P(("pb", "row"), None), P(("row", "pb"), None), P())
    out_specs = P("pb", "row")
    return jax.shard_map(local, mesh=mesh, in_specs=in_specs, out_specs=out_specs, check_vma=False)
```

profile of v0, /device:TPU:23, one launch (start us, length us, event | category | flops | bytes accessed | tf_op | source)
XLA Modules:
  0.0 300.0 jit_solution(13734901324448696239)
XLA Ops:
  6.5 0.0 all-gather.2.cloned.1.call-start
  6.5 0.7 all-gather.2.cloned.1.call-update
  7.3 19.4 %all_gather.6 = bf16[512,512]{1,0:T(8,128)(2,1)S(1)} all-gather(bf16[64,512]{1,0:T(8,128)(2,1)} %param.3), channel_id=1, replica_groups=mesh['pb'=32,'row'=8] {'row'}, dimensions={0}, use_global_device_ids=true | all-gather | bytes 589824 | tf_op jit(solution)/shard_map/all_gather | solution.py:50
  26.6 113.1 %all-gather.2.cloned.1.call-done = bf16[1536,512]{1,0:T(8,128)(2,1)} async-done(((bf16[48,512]{1,0:T(8,128)(2,1)}), bf16[1536,512]{1,0:T(8,128)(2,1)}) %all-gather.2.cloned.1.call-update) | async-done | bytes 1572880 | tf_op jit(solution)/shard_map/all_gather | solution.py:53
  139.8 2.4 fusion
  142.2 0.1 fusion.18
  142.3 0.0 copy-start
  142.3 6.7 %collective-permute-start = (f32[128,1536]{1,0:T(8,128)S(1)}, f32[128,1536]{1,0:T(8,128)S(1)}, u32[]{:S(2)}, u32[]{:S(2)}) collective-permute-start(f32[128,1536]{1,0:T(8,128)S(1)} %get-tuple-element.15), channel_id=1, source_target_pairs={{0,8},{8,16},{16,24},{24,32},{32,40},{40,48},{48,56},{56,64},{64,7... | collective-permute-start | bytes 2359304 | tf_op jit(solution)/shard_map/ppermute | solution.py:18
  149.0 1.9 collective-permute-start.1
  151.0 8.0 %collective-permute-done = f32[128,1536]{1,0:T(8,128)S(1)} collective-permute-done((f32[128,1536]{1,0:T(8,128)S(1)}, f32[128,1536]{1,0:T(8,128)S(1)}, u32[]{:S(2)}, u32[]{:S(2)}) %collective-permute-start) | collective-permute-done | bytes 786464 | tf_op jit(solution)/shard_map/ppermute | solution.py:18
  158.9 9.3 %collective-permute-done.1 = f32[128,1536]{1,0:T(8,128)S(1)} collective-permute-done((f32[128,1536]{1,0:T(8,128)S(1)}, f32[128,1536]{1,0:T(8,128)S(1)}, u32[]{:S(2)}, u32[]{:S(2)}) %collective-permute-start.1) | collective-permute-done | bytes 786464 | tf_op jit(solution)/shard_map/ppermute | solution.py:19
  168.3 0.1 pad_maximum_fusion.7
  168.3 25.3 %collective-permute-start.2 = (f32[768,128]{1,0:T(8,128)S(1)}, f32[768,128]{1,0:T(8,128)S(1)}, u32[]{:S(2)}, u32[]{:S(2)}) collective-permute-start(f32[768,128]{1,0:T(8,128)S(1)} %get-tuple-element.11), channel_id=1, source_target_pairs={{0,1},{1,2},{2,3},{3,4},{4,5},{5,6},{6,7},{8,9},{9,10},{10,11},{11... | collective-permute-start | bytes 1179656 | tf_op jit(solution)/shard_map/ppermute | solution.py:18
  193.7 1.9 collective-permute-start.3
  195.6 0.0 copy-done
  195.6 0.7 fusion.19
  196.3 2.0 collective-permute-done.2
  198.4 5.3 %collective-permute-done.3 = f32[768,128]{1,0:T(8,128)S(1)} collective-permute-done((f32[768,128]{1,0:T(8,128)S(1)}, f32[768,128]{1,0:T(8,128)S(1)}, u32[]{:S(2)}, u32[]{:S(2)}) %collective-permute-start.3) | collective-permute-done | bytes 393248 | tf_op jit(solution)/shard_map/ppermute | solution.py:19
  203.7 3.2 %maximum_maximum_fusion = (f32[768,1664]{1,0:T(8,128)S(1)}, f32[768,1664]{1,0:T(8,128)S(1)}) fusion(f32[128,1536]{1,0:T(8,128)S(1)} %collective-permute-done.1, f32[512,1536]{1,0:T(8,128)S(1)} %fusion, f32[128,1536]{1,0:T(8,128)S(1)} %collective-permute-done, f32[768,128]{1,0:T(8,128)S(1)} %collective-permute-done.2, f32[768,128]{1,0:T(8,128)S(1)} %collective-permute-done.3), kind=kLoop, calls=%fused_computation | loop fusion | flops 7667712 | bytes 15728640 | tf_op jit(solution)/shard_map/concatenate | solution.py:20
  206.8 10.2 %fusion.10 = f32[512,1536]{1,0:T(8,128)S(1)} fusion(f32[768,1664]{1,0:T(8,128)S(1)} %get-tuple-element.10, f32[768,1664]{1,0:T(8,128)S(1)} %get-tuple-element.9, f32[512,1536]{1,0:T(8,128)S(1)} %fusion, f32[]{:T(128)} %bitcast.8, f32[]{:T(128)} %bitcast.7, f32[]{:T(128)} %bitcast.6, f32[]{:T(128)} %bitcast.5, f32[]{:T(128)} %bitcast.4, f32[]{:T(128)} %bitcast.3, ...), kind=kLoop, calls=%fused_computation.23 | loop fusion | flops 11796480 | bytes 28311584 | tf_op jit(solution)/shard_map/tanh | solution.py:35
  217.0 0.1 fusion.17
  217.1 11.6 %collective-permute-start.4 = (f32[128,1536]{1,0:T(8,128)S(1)}, f32[128,1536]{1,0:T(8,128)S(1)}, u32[]{:S(2)}, u32[]{:S(2)}) collective-permute-start(f32[128,1536]{1,0:T(8,128)S(1)} %get-tuple-element.13), channel_id=1, source_target_pairs={{0,8},{8,16},{16,24},{24,32},{32,40},{40,48},{48,56},{56,64},{64,7... | collective-permute-start | bytes 2359304 | tf_op jit(solution)/shard_map/ppermute | solution.py:18
  228.7 1.9 collective-permute-start.5
  230.6 15.4 %collective-permute-done.4 = f32[128,1536]{1,0:T(8,128)S(1)} collective-permute-done((f32[128,1536]{1,0:T(8,128)S(1)}, f32[128,1536]{1,0:T(8,128)S(1)}, u32[]{:S(2)}, u32[]{:S(2)}) %collective-permute-start.4) | collective-permute-done | bytes 786464 | tf_op jit(solution)/shard_map/ppermute | solution.py:18
  246.0 11.1 %collective-permute-done.5 = f32[128,1536]{1,0:T(8,128)S(1)} collective-permute-done((f32[128,1536]{1,0:T(8,128)S(1)}, f32[128,1536]{1,0:T(8,128)S(1)}, u32[]{:S(2)}, u32[]{:S(2)}) %collective-permute-start.5) | collective-permute-done | bytes 786464 | tf_op jit(solution)/shard_map/ppermute | solution.py:19
  257.1 0.1 pad_maximum_fusion.4
  257.2 8.3 %collective-permute-start.6 = (f32[768,128]{1,0:T(8,128)S(1)}, f32[768,128]{1,0:T(8,128)S(1)}, u32[]{:S(2)}, u32[]{:S(2)}) collective-permute-start(f32[768,128]{1,0:T(8,128)S(1)} %get-tuple-element.7), channel_id=1, source_target_pairs={{0,1},{1,2},{2,3},{3,4},{4,5},{5,6},{6,7},{8,9},{9,10},{10,11},{11... | collective-permute-start | bytes 1179656 | tf_op jit(solution)/shard_map/ppermute | solution.py:18
  265.5 1.9 collective-permute-start.7
  267.4 2.8 collective-permute-done.6
  270.2 8.5 %collective-permute-done.7 = f32[768,128]{1,0:T(8,128)S(1)} collective-permute-done((f32[768,128]{1,0:T(8,128)S(1)}, f32[768,128]{1,0:T(8,128)S(1)}, u32[]{:S(2)}, u32[]{:S(2)}) %collective-permute-start.7) | collective-permute-done | bytes 393248 | tf_op jit(solution)/shard_map/ppermute | solution.py:19
  278.8 3.2 %maximum_maximum_fusion.1 = (f32[768,1664]{1,0:T(8,128)S(1)}, f32[768,1664]{1,0:T(8,128)S(1)}) fusion(f32[128,1536]{1,0:T(8,128)S(1)} %collective-permute-done.5, f32[512,1536]{1,0:T(8,128)S(1)} %fusion.10, f32[128,1536]{1,0:T(8,128)S(1)} %collective-permute-done.4, f32[768,128]{1,0:T(8,128)S(1)} %collective-permute-done.6, ...), kind=kLoop, calls=%fused_computation.2 | loop fusion | flops 7667712 | bytes 15728640 | tf_op jit(solution)/shard_map/concatenate | solution.py:20
  281.9 11.2 %fusion.2 = f32[512,1536]{1,0:T(8,128)} fusion(f32[768,1664]{1,0:T(8,128)S(1)} %get-tuple-element.6, f32[768,1664]{1,0:T(8,128)S(1)} %get-tuple-element.5, f32[512,1536]{1,0:T(8,128)S(1)} %fusion.10, f32[]{:T(128)} %bitcast.15, f32[]{:T(128)} %bitcast.14, f32[]{:T(128)} %bitcast.13, f32[]{:T(128)} %bitcast.12, f32[]{:T(128)} %bitcast.11, f32[]{:T(128)} %bitcast.10, ...), kind=kLoop, calls=%fused_computation.8 | loop fusion | flops 11796480 | bytes 28311584 | tf_op jit(solution)/shard_map/tanh | solution.py:35
Async XLA Ops:
  6.5 133.2 %all-gather.2.cloned.1.call-start = ((), (), s32[]{:S(2)}) async-start(), calls=%async_computation | async-start | bytes 1622016 | tf_op jit(solution)/shard_map/all_gather | solution.py:53
  142.3 53.3 %copy-start = (f32[2,8]{1,0:T(2,128)S(1)}, f32[2,8]{1,0:T(2,128)}, u32[]{:S(2)}) copy-start(f32[2,8]{1,0:T(2,128)} %param.5) | copy-start | bytes 196
  142.3 16.6 %collective-permute-start = (f32[128,1536]{1,0:T(8,128)S(1)}, f32[128,1536]{1,0:T(8,128)S(1)}, u32[]{:S(2)}, u32[]{:S(2)}) collective-permute-start(f32[128,1536]{1,0:T(8,128)S(1)} %get-tuple-element.15), channel_id=1, source_target_pairs={{0,8},{8,16},{16,24},{24,32},{32,40},{40,48},{48,56},{56,64},{64,7... | collective-permute-start | bytes 2359304 | tf_op jit(solution)/shard_map/ppermute | solution.py:18
  149.0 19.2 %collective-permute-start.1 = (f32[128,1536]{1,0:T(8,128)S(1)}, f32[128,1536]{1,0:T(8,128)S(1)}, u32[]{:S(2)}, u32[]{:S(2)}) collective-permute-start(f32[128,1536]{1,0:T(8,128)S(1)} %get-tuple-element.16), channel_id=1, source_target_pairs={{8,0},{16,8},{24,16},{32,24},{40,32},{48,40},{56,48},{64,56},{72,6... | collective-permute-start | bytes 2359304 | tf_op jit(solution)/shard_map/ppermute | solution.py:19
  168.3 30.0 %collective-permute-start.2 = (f32[768,128]{1,0:T(8,128)S(1)}, f32[768,128]{1,0:T(8,128)S(1)}, u32[]{:S(2)}, u32[]{:S(2)}) collective-permute-start(f32[768,128]{1,0:T(8,128)S(1)} %get-tuple-element.11), channel_id=1, source_target_pairs={{0,1},{1,2},{2,3},{3,4},{4,5},{5,6},{6,7},{8,9},{9,10},{10,11},{11... | collective-permute-start | bytes 1179656 | tf_op jit(solution)/shard_map/ppermute | solution.py:18
  193.7 10.0 %collective-permute-start.3 = (f32[768,128]{1,0:T(8,128)S(1)}, f32[768,128]{1,0:T(8,128)S(1)}, u32[]{:S(2)}, u32[]{:S(2)}) collective-permute-start(f32[768,128]{1,0:T(8,128)S(1)} %get-tuple-element.12), channel_id=1, source_target_pairs={{1,0},{2,1},{3,2},{4,3},{5,4},{6,5},{7,6},{9,8},{10,9},{11,10},{12... | collective-permute-start | bytes 1179656 | tf_op jit(solution)/shard_map/ppermute | solution.py:19
  217.1 28.9 %collective-permute-start.4 = (f32[128,1536]{1,0:T(8,128)S(1)}, f32[128,1536]{1,0:T(8,128)S(1)}, u32[]{:S(2)}, u32[]{:S(2)}) collective-permute-start(f32[128,1536]{1,0:T(8,128)S(1)} %get-tuple-element.13), channel_id=1, source_target_pairs={{0,8},{8,16},{16,24},{24,32},{32,40},{40,48},{48,56},{56,64},{64,7... | collective-permute-start | bytes 2359304 | tf_op jit(solution)/shard_map/ppermute | solution.py:18
  228.7 28.5 %collective-permute-start.5 = (f32[128,1536]{1,0:T(8,128)S(1)}, f32[128,1536]{1,0:T(8,128)S(1)}, u32[]{:S(2)}, u32[]{:S(2)}) collective-permute-start(f32[128,1536]{1,0:T(8,128)S(1)} %get-tuple-element.14), channel_id=1, source_target_pairs={{8,0},{16,8},{24,16},{32,24},{40,32},{48,40},{56,48},{64,56},{72,6... | collective-permute-start | bytes 2359304 | tf_op jit(solution)/shard_map/ppermute | solution.py:19
  257.2 13.0 %collective-permute-start.6 = (f32[768,128]{1,0:T(8,128)S(1)}, f32[768,128]{1,0:T(8,128)S(1)}, u32[]{:S(2)}, u32[]{:S(2)}) collective-permute-start(f32[768,128]{1,0:T(8,128)S(1)} %get-tuple-element.7), channel_id=1, source_target_pairs={{0,1},{1,2},{2,3},{3,4},{4,5},{5,6},{6,7},{8,9},{9,10},{10,11},{11... | collective-permute-start | bytes 1179656 | tf_op jit(solution)/shard_map/ppermute | solution.py:18
  265.5 13.3 %collective-permute-start.7 = (f32[768,128]{1,0:T(8,128)S(1)}, f32[768,128]{1,0:T(8,128)S(1)}, u32[]{:S(2)}, u32[]{:S(2)}) collective-permute-start(f32[768,128]{1,0:T(8,128)S(1)} %get-tuple-element.8), channel_id=1, source_target_pairs={{1,0},{2,1},{3,2},{4,3},{5,4},{6,5},{7,6},{9,8},{10,9},{11,10},{12... | collective-permute-start | bytes 1179656 | tf_op jit(solution)/shard_map/ppermute | solution.py:19
Sparse Core Ops, SparseCore 0:
  9.1 130.5 all-gather.1
where the time goes:
time: 300 us
  waiting for transfers between devices  176 us (59%)
  starting transfers between devices  59.6 us (20%)
  other arithmetic  27.8 us (9%)
  blocking collectives  19.4 us (6%)
  between operations  13.5 us (4%)
    all_gather x1, waiting for transfers between devices, local(): lax.all_gather(ref_desc, 'pb', axis=0, tiled=True)  113 us
    ppermute x4, starting transfers between devices, padded(): before = lax.ppermute(last, axis, up)  51.9 us
    ppermute x4, waiting for transfers between devices, padded(): after = lax.ppermute(leading, axis, down)  34.3 us
    ppermute x4, waiting for transfers between devices, padded(): before = lax.ppermute(last, axis, up)  28.2 us
    tanh x2, other arithmetic, diagonal_pass(): return jnp.tanh(total_reach)  21.4 us
    all_gather x1, blocking collectives, local(): queries = lax.all_gather(query_desc, 'row', axis=0, tiled=True)  19.4 us
    ppermute x4, starting transfers between devices, padded(): after = lax.ppermute(leading, axis, down)  7.68 us
    concatenate x2, other arithmetic, padded(): value = jnp.concatenate([before, value, after], axis=dim)  6.3 us
  transfers between devices with their start and end apart: 9, of which 9 were waited for; matrix products, arithmetic and copies ran while one was open for 0% of the time, Pallas kernels for 0%

commit v1 on v0

--- a/solution.py
+++ b/solution.py
@@ -50,7 +50,12 @@
     queries = lax.all_gather(query_desc, "row", axis=0, tiled=True)
     rows = queries.shape[0]
     cols = ref_desc.shape[0] * lax.axis_size("pb")
-    sim = inner_scores(queries, lax.all_gather(ref_desc, "pb", axis=0, tiled=True))
+    sim = inner_scores(
+        queries,
+        jnp.concatenate(
+            lax.all_to_all(jnp.stack([ref_desc] * lax.axis_size("pb")), "pb", 0, 0), axis=0
+        ),
+    )
     base = jnp.tanh(sim * scale)
     first = diagonal_pass(pass_rims(base), taps[0], rows, cols)
     return diagonal_pass(pass_rims(first), taps[1], rows, cols)

time: 300 us -> 186 us (0.62)
  waiting for transfers between devices: 176 us -> 75.4 us
  starting transfers between devices: 59.6 us -> 43.9 us
  blocking collectives: 19.4 us -> 33.3 us
  between operations: 13.5 us -> 0.16 us
    all_gather x1 -> x0, waiting for transfers between devices: 113 us -> none  [local(): lax.all_gather(ref_desc, 'pb', axis=0, tiled=True)]
    ppermute x4, starting transfers between devices: 51.9 us -> 27.6 us  [padded(): before = lax.ppermute(last, axis, up)]
    all_gather x1, blocking collectives: 19.4 us -> 33.3 us  [local(): queries = lax.all_gather(query_desc, 'row', axis=0, tiled=True)]
    all_to_all x0 -> x1, starting transfers between devices: none -> 8.2 us  [local(): lax.all_to_all(jnp.stack([ref_desc] * lax.axis_size('pb')), 'pb', 0, 0)]
    ppermute x4, waiting for transfers between devices: 28.2 us -> 35.8 us  [padded(): before = lax.ppermute(last, axis, up)]
    ppermute x4, waiting for transfers between devices: 34.3 us -> 39.7 us  [padded(): after = lax.ppermute(leading, axis, down)]
  transfers between devices with their start and end apart: 9 -> 9, of which waited for: 9 -> 8; matrix products, arithmetic and copies ran while one was open for 0% -> 0% of each run, Pallas kernels for 0% -> 0%
where the time goes in v1:
time: 186 us; the launch traced here: 185 us
  waiting for transfers between devices  75.4 us (41%)
  starting transfers between devices  43.9 us (24%)
  blocking collectives  33.3 us (18%)
  other arithmetic  27.8 us (15%)
  local copies, waits for them, and re-layouts  3.09 us (2%)
    ppermute x4, waiting for transfers between devices, padded(): after = lax.ppermute(leading, axis, down)  39.7 us
    ppermute x4, waiting for transfers between devices, padded(): before = lax.ppermute(last, axis, up)  35.8 us
    all_gather x1, blocking collectives, local(): queries = lax.all_gather(query_desc, 'row', axis=0, tiled=True)  33.3 us
    ppermute x4, starting transfers between devices, padded(): before = lax.ppermute(last, axis, up)  27.6 us
    tanh x2, other arithmetic, diagonal_pass(): return jnp.tanh(total_reach)  21.4 us
    all_to_all x1, starting transfers between devices, local(): lax.all_to_all(jnp.stack([ref_desc] * lax.axis_size('pb')), 'pb', 0, 0)  8.2 us
    ppermute x4, starting transfers between devices, padded(): after = lax.ppermute(leading, axis, down)  8.11 us
    concatenate x2, other arithmetic, padded(): value = jnp.concatenate([before, value, after], axis=dim)  6.3 us
  transfers between devices with their start and end apart: 9, of which 8 were waited for; matrix products, arithmetic and copies ran while one was open for 0% of the time, Pallas kernels for 0%

profile of v1, /device:TPU:23, one launch (start us, length us, event | category | flops | bytes accessed | tf_op | source)
XLA Modules:
  0.0 184.8 jit_solution(12857873339579453230)
XLA Ops:
  0.0 0.0 copy-start
  0.0 2.1 %stack.2 = bf16[32,48,512]{2,1,0:T(8,128)(2,1)} broadcast(bf16[48,512]{1,0:T(8,128)(2,1)} %param.4), dimensions={1,2} | broadcast | bytes 1622016 | tf_op jit(solution)/shard_map/stack | solution.py:56
  2.2 8.2 %all-to-all-start = ((bf16[32,48,512]{2,1,0:T(8,128)(2,1)}), bf16[32,48,512]{2,1,0:T(8,128)(2,1)S(1)}, u32[]{:S(2)}, u32[]{:S(2)}) async-start(bf16[32,48,512]{2,1,0:T(8,128)(2,1)} %stack.2), calls=%async_computation | async-start | bytes 3145728 | tf_op jit(solution)/shard_map/all_to_all | solution.py:56
  10.4 0.0 copy-done
  10.4 33.3 %all_gather.3 = bf16[512,512]{1,0:T(8,128)(2,1)S(1)} all-gather(bf16[64,512]{1,0:T(8,128)(2,1)S(1)} %copy-done), channel_id=1, replica_groups=mesh['pb'=32,'row'=8] {'row'}, dimensions={0}, use_global_device_ids=true | all-gather | bytes 589824 | tf_op jit(solution)/shard_map/all_gather | solution.py:50
  43.7 0.0 all-to-all-done
  43.7 1.0 fusion
  44.7 0.1 fusion.18
  44.8 0.0 copy-start.1
  44.8 3.8 %collective-permute-start = (f32[128,1536]{1,0:T(8,128)S(1)}, f32[128,1536]{1,0:T(8,128)S(1)}, u32[]{:S(2)}, u32[]{:S(2)}) collective-permute-start(f32[128,1536]{1,0:T(8,128)S(1)} %get-tuple-element.15), channel_id=1, source_target_pairs={{0,8},{8,16},{16,24},{24,32},{32,40},{40,48},{48,56},{56,64},{64,7... | collective-permute-start | bytes 2359304 | tf_op jit(solution)/shard_map/ppermute | solution.py:18
  48.7 2.3 %collective-permute-start.1 = (f32[128,1536]{1,0:T(8,128)S(1)}, f32[128,1536]{1,0:T(8,128)S(1)}, u32[]{:S(2)}, u32[]{:S(2)}) collective-permute-start(f32[128,1536]{1,0:T(8,128)S(1)} %get-tuple-element.16), channel_id=1, source_target_pairs={{8,0},{16,8},{24,16},{32,24},{40,32},{48,40},{56,48},{64,56},{72,6... | collective-permute-start | bytes 2359304 | tf_op jit(solution)/shard_map/ppermute | solution.py:19
  51.0 15.5 %collective-permute-done = f32[128,1536]{1,0:T(8,128)S(1)} collective-permute-done((f32[128,1536]{1,0:T(8,128)S(1)}, f32[128,1536]{1,0:T(8,128)S(1)}, u32[]{:S(2)}, u32[]{:S(2)}) %collective-permute-start) | collective-permute-done | bytes 786464 | tf_op jit(solution)/shard_map/ppermute | solution.py:18
  66.5 16.5 %collective-permute-done.1 = f32[128,1536]{1,0:T(8,128)S(1)} collective-permute-done((f32[128,1536]{1,0:T(8,128)S(1)}, f32[128,1536]{1,0:T(8,128)S(1)}, u32[]{:S(2)}, u32[]{:S(2)}) %collective-permute-start.1) | collective-permute-done | bytes 786464 | tf_op jit(solution)/shard_map/ppermute | solution.py:19
  83.0 0.1 pad_maximum_fusion.7
  83.1 5.5 %collective-permute-start.2 = (f32[768,128]{1,0:T(8,128)S(1)}, f32[768,128]{1,0:T(8,128)S(1)}, u32[]{:S(2)}, u32[]{:S(2)}) collective-permute-start(f32[768,128]{1,0:T(8,128)S(1)} %get-tuple-element.11), channel_id=1, source_target_pairs={{0,1},{1,2},{2,3},{3,4},{4,5},{5,6},{6,7},{8,9},{9,10},{10,11},{11... | collective-permute-start | bytes 1179656 | tf_op jit(solution)/shard_map/ppermute | solution.py:18
  88.6 1.9 %collective-permute-start.3 = (f32[768,128]{1,0:T(8,128)S(1)}, f32[768,128]{1,0:T(8,128)S(1)}, u32[]{:S(2)}, u32[]{:S(2)}) collective-permute-start(f32[768,128]{1,0:T(8,128)S(1)} %get-tuple-element.12), channel_id=1, source_target_pairs={{1,0},{2,1},{3,2},{4,3},{5,4},{6,5},{7,6},{9,8},{10,9},{11,10},{12... | collective-permute-start | bytes 1179656 | tf_op jit(solution)/shard_map/ppermute | solution.py:19
  90.6 0.0 copy-done.1
  90.6 0.7 fusion.19
  91.3 2.0 %collective-permute-done.2 = f32[768,128]{1,0:T(8,128)S(1)} collective-permute-done((f32[768,128]{1,0:T(8,128)S(1)}, f32[768,128]{1,0:T(8,128)S(1)}, u32[]{:S(2)}, u32[]{:S(2)}) %collective-permute-start.2) | collective-permute-done | bytes 393248 | tf_op jit(solution)/shard_map/ppermute | solution.py:18
  93.3 5.3 %collective-permute-done.3 = f32[768,128]{1,0:T(8,128)S(1)} collective-permute-done((f32[768,128]{1,0:T(8,128)S(1)}, f32[768,128]{1,0:T(8,128)S(1)}, u32[]{:S(2)}, u32[]{:S(2)}) %collective-permute-start.3) | collective-permute-done | bytes 393248 | tf_op jit(solution)/shard_map/ppermute | solution.py:19
  98.6 3.2 %maximum_maximum_fusion = (f32[768,1664]{1,0:T(8,128)S(1)}, f32[768,1664]{1,0:T(8,128)S(1)}) fusion(f32[128,1536]{1,0:T(8,128)S(1)} %collective-permute-done.1, f32[512,1536]{1,0:T(8,128)S(1)} %fusion, f32[128,1536]{1,0:T(8,128)S(1)} %collective-permute-done, f32[768,128]{1,0:T(8,128)S(1)} %collective-permute-done.2, f32[768,128]{1,0:T(8,128)S(1)} %collective-permute-done.3), kind=kLoop, calls=%fused_computation | loop fusion | flops 7667712 | bytes 15728640 | tf_op jit(solution)/shard_map/concatenate | solution.py:20
  101.8 10.2 %fusion.10 = f32[512,1536]{1,0:T(8,128)S(1)} fusion(f32[768,1664]{1,0:T(8,128)S(1)} %get-tuple-element.10, f32[768,1664]{1,0:T(8,128)S(1)} %get-tuple-element.9, f32[512,1536]{1,0:T(8,128)S(1)} %fusion, f32[]{:T(128)} %bitcast.9, f32[]{:T(128)} %bitcast.8, f32[]{:T(128)} %bitcast.7, f32[]{:T(128)} %bitcast.6, f32[]{:T(128)} %bitcast.5, f32[]{:T(128)} %bitcast.4, ...), kind=kLoop, calls=%fused_computation.23 | loop fusion | flops 11796480 | bytes 28311584 | tf_op jit(solution)/shard_map/tanh | solution.py:35
  112.0 0.1 fusion.17
  112.1 8.1 %collective-permute-start.4 = (f32[128,1536]{1,0:T(8,128)S(1)}, f32[128,1536]{1,0:T(8,128)S(1)}, u32[]{:S(2)}, u32[]{:S(2)}) collective-permute-start(f32[128,1536]{1,0:T(8,128)S(1)} %get-tuple-element.13), channel_id=1, source_target_pairs={{0,8},{8,16},{16,24},{24,32},{32,40},{40,48},{48,56},{56,64},{64,7... | collective-permute-start | bytes 2359304 | tf_op jit(solution)/shard_map/ppermute | solution.py:18
  120.2 1.9 %collective-permute-start.5 = (f32[128,1536]{1,0:T(8,128)S(1)}, f32[128,1536]{1,0:T(8,128)S(1)}, u32[]{:S(2)}, u32[]{:S(2)}) collective-permute-start(f32[128,1536]{1,0:T(8,128)S(1)} %get-tuple-element.14), channel_id=1, source_target_pairs={{8,0},{16,8},{24,16},{32,24},{40,32},{48,40},{56,48},{64,56},{72,6... | collective-permute-start | bytes 2359304 | tf_op jit(solution)/shard_map/ppermute | solution.py:19
  122.1 15.4 %collective-permute-done.4 = f32[128,1536]{1,0:T(8,128)S(1)} collective-permute-done((f32[128,1536]{1,0:T(8,128)S(1)}, f32[128,1536]{1,0:T(8,128)S(1)}, u32[]{:S(2)}, u32[]{:S(2)}) %collective-permute-start.4) | collective-permute-done | bytes 786464 | tf_op jit(solution)/shard_map/ppermute | solution.py:18
  137.5 9.1 %collective-permute-done.5 = f32[128,1536]{1,0:T(8,128)S(1)} collective-permute-done((f32[128,1536]{1,0:T(8,128)S(1)}, f32[128,1536]{1,0:T(8,128)S(1)}, u32[]{:S(2)}, u32[]{:S(2)}) %collective-permute-start.5) | collective-permute-done | bytes 786464 | tf_op jit(solution)/shard_map/ppermute | solution.py:19
  146.7 0.1 pad_maximum_fusion.4
  146.7 10.2 %collective-permute-start.6 = (f32[768,128]{1,0:T(8,128)S(1)}, f32[768,128]{1,0:T(8,128)S(1)}, u32[]{:S(2)}, u32[]{:S(2)}) collective-permute-start(f32[768,128]{1,0:T(8,128)S(1)} %get-tuple-element.7), channel_id=1, source_target_pairs={{0,1},{1,2},{2,3},{3,4},{4,5},{5,6},{6,7},{8,9},{9,10},{10,11},{11... | collective-permute-start | bytes 1179656 | tf_op jit(solution)/shard_map/ppermute | solution.py:18
  156.9 1.9 %collective-permute-start.7 = (f32[768,128]{1,0:T(8,128)S(1)}, f32[768,128]{1,0:T(8,128)S(1)}, u32[]{:S(2)}, u32[]{:S(2)}) collective-permute-start(f32[768,128]{1,0:T(8,128)S(1)} %get-tuple-element.8), channel_id=1, source_target_pairs={{1,0},{2,1},{3,2},{4,3},{5,4},{6,5},{7,6},{9,8},{10,9},{11,10},{12... | collective-permute-start | bytes 1179656 | tf_op jit(solution)/shard_map/ppermute | solution.py:19
  158.8 2.8 %collective-permute-done.6 = f32[768,128]{1,0:T(8,128)S(1)} collective-permute-done((f32[768,128]{1,0:T(8,128)S(1)}, f32[768,128]{1,0:T(8,128)S(1)}, u32[]{:S(2)}, u32[]{:S(2)}) %collective-permute-start.6) | collective-permute-done | bytes 393248 | tf_op jit(solution)/shard_map/ppermute | solution.py:18
  161.6 8.7 %collective-permute-done.7 = f32[768,128]{1,0:T(8,128)S(1)} collective-permute-done((f32[768,128]{1,0:T(8,128)S(1)}, f32[768,128]{1,0:T(8,128)S(1)}, u32[]{:S(2)}, u32[]{:S(2)}) %collective-permute-start.7) | collective-permute-done | bytes 393248 | tf_op jit(solution)/shard_map/ppermute | solution.py:19
  170.3 3.2 %maximum_maximum_fusion.1 = (f32[768,1664]{1,0:T(8,128)S(1)}, f32[768,1664]{1,0:T(8,128)S(1)}) fusion(f32[128,1536]{1,0:T(8,128)S(1)} %collective-permute-done.5, f32[512,1536]{1,0:T(8,128)S(1)} %fusion.10, f32[128,1536]{1,0:T(8,128)S(1)} %collective-permute-done.4, f32[768,128]{1,0:T(8,128)S(1)} %collective-permute-done.6, ...), kind=kLoop, calls=%fused_computation.2 | loop fusion | flops 7667712 | bytes 15728640 | tf_op jit(solution)/shard_map/concatenate | solution.py:20
  173.5 11.2 %fusion.2 = f32[512,1536]{1,0:T(8,128)} fusion(f32[768,1664]{1,0:T(8,128)S(1)} %get-tuple-element.6, f32[768,1664]{1,0:T(8,128)S(1)} %get-tuple-element.5, f32[512,1536]{1,0:T(8,128)S(1)} %fusion.10, f32[]{:T(128)} %bitcast.16, f32[]{:T(128)} %bitcast.15, f32[]{:T(128)} %bitcast.14, f32[]{:T(128)} %bitcast.13, f32[]{:T(128)} %bitcast.12, f32[]{:T(128)} %bitcast.11, ...), kind=kLoop, calls=%fused_computation.8 | loop fusion | flops 11796480 | bytes 28311584 | tf_op jit(solution)/shard_map/tanh | solution.py:35
Async XLA Ops:
  0.0 10.4 %copy-start = (bf16[64,512]{1,0:T(8,128)(2,1)S(1)}, bf16[64,512]{1,0:T(8,128)(2,1)}, u32[]{:S(2)}) copy-start(bf16[64,512]{1,0:T(8,128)(2,1)} %param.3) | copy-start | bytes 196612
  2.2 41.5 %all-to-all-start = ((bf16[32,48,512]{2,1,0:T(8,128)(2,1)}), bf16[32,48,512]{2,1,0:T(8,128)(2,1)S(1)}, u32[]{:S(2)}, u32[]{:S(2)}) async-start(bf16[32,48,512]{2,1,0:T(8,128)(2,1)} %stack.2), calls=%async_computation | async-start | bytes 3145728 | tf_op jit(solution)/shard_map/all_to_all | solution.py:56
  44.8 45.8 %copy-start.1 = (f32[2,8]{1,0:T(2,128)S(1)}, f32[2,8]{1,0:T(2,128)}, u32[]{:S(2)}) copy-start(f32[2,8]{1,0:T(2,128)} %param.5) | copy-start | bytes 196
  44.8 21.7 %collective-permute-start = (f32[128,1536]{1,0:T(8,128)S(1)}, f32[128,1536]{1,0:T(8,128)S(1)}, u32[]{:S(2)}, u32[]{:S(2)}) collective-permute-start(f32[128,1536]{1,0:T(8,128)S(1)} %get-tuple-element.15), channel_id=1, source_target_pairs={{0,8},{8,16},{16,24},{24,32},{32,40},{40,48},{48,56},{56,64},{64,7... | collective-permute-start | bytes 2359304 | tf_op jit(solution)/shard_map/ppermute | solution.py:18
  48.7 34.4 %collective-permute-start.1 = (f32[128,1536]{1,0:T(8,128)S(1)}, f32[128,1536]{1,0:T(8,128)S(1)}, u32[]{:S(2)}, u32[]{:S(2)}) collective-permute-start(f32[128,1536]{1,0:T(8,128)S(1)} %get-tuple-element.16), channel_id=1, source_target_pairs={{8,0},{16,8},{24,16},{32,24},{40,32},{48,40},{56,48},{64,56},{72,6... | collective-permute-start | bytes 2359304 | tf_op jit(solution)/shard_map/ppermute | solution.py:19
  83.1 10.2 %collective-permute-start.2 = (f32[768,128]{1,0:T(8,128)S(1)}, f32[768,128]{1,0:T(8,128)S(1)}, u32[]{:S(2)}, u32[]{:S(2)}) collective-permute-start(f32[768,128]{1,0:T(8,128)S(1)} %get-tuple-element.11), channel_id=1, source_target_pairs={{0,1},{1,2},{2,3},{3,4},{4,5},{5,6},{6,7},{8,9},{9,10},{10,11},{11... | collective-permute-start | bytes 1179656 | tf_op jit(solution)/shard_map/ppermute | solution.py:18
  88.6 10.0 %collective-permute-start.3 = (f32[768,128]{1,0:T(8,128)S(1)}, f32[768,128]{1,0:T(8,128)S(1)}, u32[]{:S(2)}, u32[]{:S(2)}) collective-permute-start(f32[768,128]{1,0:T(8,128)S(1)} %get-tuple-element.12), channel_id=1, source_target_pairs={{1,0},{2,1},{3,2},{4,3},{5,4},{6,5},{7,6},{9,8},{10,9},{11,10},{12... | collective-permute-start | bytes 1179656 | tf_op jit(solution)/shard_map/ppermute | solution.py:19
  112.1 25.4 %collective-permute-start.4 = (f32[128,1536]{1,0:T(8,128)S(1)}, f32[128,1536]{1,0:T(8,128)S(1)}, u32[]{:S(2)}, u32[]{:S(2)}) collective-permute-start(f32[128,1536]{1,0:T(8,128)S(1)} %get-tuple-element.13), channel_id=1, source_target_pairs={{0,8},{8,16},{16,24},{24,32},{32,40},{40,48},{48,56},{56,64},{64,7... | collective-permute-start | bytes 2359304 | tf_op jit(solution)/shard_map/ppermute | solution.py:18
  120.2 26.5 %collective-permute-start.5 = (f32[128,1536]{1,0:T(8,128)S(1)}, f32[128,1536]{1,0:T(8,128)S(1)}, u32[]{:S(2)}, u32[]{:S(2)}) collective-permute-start(f32[128,1536]{1,0:T(8,128)S(1)} %get-tuple-element.14), channel_id=1, source_target_pairs={{8,0},{16,8},{24,16},{32,24},{40,32},{48,40},{56,48},{64,56},{72,6... | collective-permute-start | bytes 2359304 | tf_op jit(solution)/shard_map/ppermute | solution.py:19
  146.7 14.9 %collective-permute-start.6 = (f32[768,128]{1,0:T(8,128)S(1)}, f32[768,128]{1,0:T(8,128)S(1)}, u32[]{:S(2)}, u32[]{:S(2)}) collective-permute-start(f32[768,128]{1,0:T(8,128)S(1)} %get-tuple-element.7), channel_id=1, source_target_pairs={{0,1},{1,2},{2,3},{3,4},{4,5},{5,6},{6,7},{8,9},{9,10},{10,11},{11... | collective-permute-start | bytes 1179656 | tf_op jit(solution)/shard_map/ppermute | solution.py:18
  156.9 13.5 %collective-permute-start.7 = (f32[768,128]{1,0:T(8,128)S(1)}, f32[768,128]{1,0:T(8,128)S(1)}, u32[]{:S(2)}, u32[]{:S(2)}) collective-permute-start(f32[768,128]{1,0:T(8,128)S(1)} %get-tuple-element.8), channel_id=1, source_target_pairs={{1,0},{2,1},{3,2},{4,3},{5,4},{6,5},{7,6},{9,8},{10,9},{11,10},{12... | collective-permute-start | bytes 1179656 | tf_op jit(solution)/shard_map/ppermute | solution.py:19
